TPU v7x, 32 devices: a whole 2x2x4 slice. The times are simulated.
32 devices in a mesh: section: 2 (over y), tensor: 4 (over z), dp: 4 (over x, core).
Axes of the slice: x: 2, y: 2, z: 4, core: 2. Of those that a mesh axis runs over, the one named last changes fastest.
Arguments:
- tokens_in: bfloat16 [4, 256, 4, 2048], P(None, 'tensor', 'dp'), may hold values from -6 to 6
- cotangent: bfloat16 [4, 256, 4, 2048], P(None, 'tensor', 'dp'), may hold values from -6 to 6
- ln1_gain: bfloat16 [2, 2048], P('section'), may hold values from 0.5 to 1.5
- ln1_bias: bfloat16 [2, 2048], P('section'), may hold values from -1 to 1
- q_weight: bfloat16 [2, 2048, 2048], P('section', None, 'tensor'), may hold values from -0.125 to 0.125
- q_bias: bfloat16 [2, 2048], P('section', 'tensor'), may hold values from -1.5 to 1.5
- kv_weight: bfloat16 [2, 2048, 256], P('section'), may hold values from -0.125 to 0.125
- v_bias: bfloat16 [2, 128], P('section'), may hold values from -0.25 to 0.25
- o_weight: bfloat16 [2, 2048, 2048], P('section', 'tensor'), may hold values from -1.5 to 1.5
- o_bias: bfloat16 [2, 2048], P('section'), may hold values from -1.5 to 1.5
- ln2_gain: bfloat16 [2, 2048], P('section'), may hold values from 0.5 to 1.5
- ln2_bias: bfloat16 [2, 2048], P('section'), may hold values from -1 to 1
- up_weight: bfloat16 [2, 2048, 8192], P('section', None, 'tensor'), may hold values from -0.125 to 0.125
- up_bias: bfloat16 [2, 8192], P('section', 'tensor'), may hold values from -1.5 to 1.5
- down_weight: bfloat16 [2, 8192, 2048], P('section', 'tensor'), may hold values from -0.0625 to 0.0625
- down_bias: bfloat16 [2, 2048], P('section'), may hold values from -1.5 to 1.5
Outputs:
- layer_out: bfloat16 [2, 4, 256, 4, 2048], P('section', None, 'tensor', 'dp')
- input_grad: float32 [2, 4, 256, 4, 2048], P('section', None, 'tensor', 'dp')
- ln1_gain_grad: float32 [2, 2048], P('section')
- ln1_bias_grad: float32 [2, 2048], P('section')
- q_weight_grad: float32 [2, 2048, 2048], P('section', None, 'tensor')
- q_bias_grad: float32 [2, 2048], P('section', 'tensor')
- kv_weight_grad: float32 [2, 2048, 256], P('section')
- v_bias_grad: float32 [2, 128], P('section')
- o_weight_grad: float32 [2, 2048, 2048], P('section', 'tensor')
- o_bias_grad: float32 [2, 2048], P('section')
- ln2_gain_grad: float32 [2, 2048], P('section')
- ln2_bias_grad: float32 [2, 2048], P('section')
- up_weight_grad: float32 [2, 2048, 8192], P('section', None, 'tensor')
- up_bias_grad: float32 [2, 8192], P('section', 'tensor')
- down_weight_grad: float32 [2, 8192, 2048], P('section', 'tensor')
- down_bias_grad: float32 [2, 2048], P('section')
All inputs are finite; a program needn't handle non-finite values.
Results may differ from a plain program's by a relative error of at most 0.022.
Values may be sent and summed in bfloat16 or wider, within the bound.
A program may use at most 512 MiB of HBM per device.

v0:
```python
import math
import jax
import jax.numpy as jnp
from jax import lax
from jax.sharding import PartitionSpec as P

HD = 128


def from_behind(block, axis, distance):
    devices = range(lax.axis_size(axis))
    route = [(i - distance, i) for i in devices if i - distance in devices]
    return lax.ppermute(block, axis, route)


def for_sending(shard):
    return jax.tree.map(lambda a: a.astype(jnp.bfloat16) if a.dtype == jnp.float32 else a, shard)


def layer_norm(values, gain_vec, bias_vec):
    row_mean = jnp.mean(values, axis=-1, keepdims=True)
    centred = values - row_mean
    row_var = jnp.mean(centred * centred, axis=-1, keepdims=True)
    return centred * lax.rsqrt(row_var + 1e-05) * gain_vec + bias_vec


def gelu_tanh(values):
    return jax.nn.gelu(values, approximate=True)


def gather_rows(own_rows):
    return lax.all_gather(own_rows, "tensor", axis=0, tiled=True)


def sum_rows(term_fn, own_count):
    return lax.psum_scatter(
        term_fn(jnp.int32(0), own_count * lax.axis_size("tensor")).astype(jnp.bfloat16),
        "tensor",
        scatter_dimension=0,
        tiled=True,
    ).astype(jnp.float32)


def on_device(
    tokens_in,
    cotangent,
    ln1_gain,
    ln1_bias,
    q_weight,
    q_bias,
    kv_weight,
    v_bias,
    o_weight,
    o_bias,
    ln2_gain,
    ln2_bias,
    up_weight,
    up_bias,
    down_weight,
    down_bias,
):
    f32 = jnp.float32
    bf16 = jnp.bfloat16
    section = lax.axis_index("section")
    tensor_count = lax.axis_size("tensor")
    tensor_rank = lax.axis_index("tensor")
    gain_one = ln1_gain[0].astype(f32)
    bias_one = ln1_bias[0].astype(f32)
    w_query = q_weight[0]
    b_query = q_bias[0].astype(f32)
    w_pairs = kv_weight[0]
    pair_bias = jnp.concatenate([jnp.zeros((HD,), f32), v_bias[0].astype(f32)])
    w_out = o_weight[0]
    b_out = o_bias[0].astype(f32)
    gain_two = ln2_gain[0].astype(f32)
    bias_two = ln2_bias[0].astype(f32)
    w_up = up_weight[0]
    b_up = up_bias[0].astype(f32)
    w_down = down_weight[0]
    b_down = down_bias[0].astype(f32)
    blocks, own_count, seq_count, model_dim = tokens_in.shape
    block_len = own_count * tensor_count
    total_len = blocks * block_len
    heads_local = w_query.shape[1] // HD
    ff_local = w_up.shape[1]
    score_scale = 1.0 / math.sqrt(HD)
    positions = jnp.arange(total_len, dtype=jnp.int32)
    own_start = tensor_rank * own_count
    kept_normed = jnp.zeros((blocks, block_len, seq_count, model_dim), bf16)
    kept_query = jnp.zeros((blocks, block_len, seq_count, heads_local * HD), bf16)
    kept_attended = jnp.zeros((blocks, block_len, seq_count, heads_local * HD), bf16)
    kept_logsum = jnp.zeros((blocks, seq_count, block_len, heads_local), f32)
    kv_cache = jnp.zeros((total_len, seq_count, 2 * HD), bf16)
    kept_input = jnp.zeros((blocks, own_count, seq_count, model_dim), f32)
    kept_hidden = jnp.zeros((blocks, own_count, seq_count, model_dim), f32)
    kept_normed_two = jnp.zeros((blocks, block_len, seq_count, model_dim), bf16)
    kept_pre = jnp.zeros((blocks, block_len, seq_count, ff_local), f32)
    outputs = jnp.zeros((blocks, own_count, seq_count, model_dim), bf16)
    received = jnp.zeros((own_count, seq_count, model_dim), f32)
    for turn in range(blocks + 1):
        block_index = jnp.clip(turn - section, 0, blocks - 1)
        from_input = lax.dynamic_index_in_dim(tokens_in, block_index, 0, keepdims=False).astype(f32)
        layer_input = jnp.where(section == 0, from_input, received)
        normed = gather_rows(layer_norm(layer_input, gain_one, bias_one).astype(bf16))
        query = (
            jnp.einsum("rsd,de->rse", normed, w_query, preferred_element_type=f32) + b_query
        ).astype(bf16)
        pairs = jnp.einsum("rsd,dc->rsc", normed, w_pairs, preferred_element_type=f32) + pair_bias
        kv_cache = lax.dynamic_update_slice_in_dim(
            kv_cache, pairs.astype(bf16), block_index * block_len, 0
        )
        key_rows = kv_cache[..., :HD]
        value_rows = kv_cache[..., HD:]
        visible = positions < (block_index + 1) * block_len
        query_heads = query.reshape(block_len, seq_count, heads_local, HD)
        scores = (
            jnp.einsum("qshd,ksd->sqhk", query_heads, key_rows, preferred_element_type=f32)
            * score_scale
        )
        scores = jnp.where(visible, scores, -1e30)
        row_top = jnp.max(scores, axis=-1, keepdims=True)
        exponent = jnp.exp(scores - row_top)
        row_total = jnp.sum(exponent, axis=-1, keepdims=True)
        log_total = (row_top + jnp.log(row_total))[..., 0]
        weights_low = (exponent / row_total).astype(bf16)
        attended = jnp.einsum("sqhk,ksd->qshd", weights_low, value_rows, preferred_element_type=f32)
        attended = attended.reshape(block_len, seq_count, heads_local * HD).astype(bf16)

        def attention_term(start, count, attended=attended):
            return jnp.einsum("rse,ed->rsd", attended, w_out, preferred_element_type=f32)

        hidden = layer_input + sum_rows(attention_term, own_count) + b_out
        normed_two = gather_rows(layer_norm(hidden, gain_two, bias_two).astype(bf16))
        pre_active = jnp.einsum("rsd,df->rsf", normed_two, w_up, preferred_element_type=f32) + b_up
        active = gelu_tanh(pre_active).astype(bf16)

        def feed_term(start, count, active=active):
            return jnp.einsum("rsf,fd->rsd", active, w_down, preferred_element_type=f32)

        result_low = (hidden + sum_rows(feed_term, own_count) + b_down).astype(bf16)
        kept_normed = lax.dynamic_update_index_in_dim(kept_normed, normed, block_index, 0)
        kept_query = lax.dynamic_update_index_in_dim(kept_query, query, block_index, 0)
        kept_attended = lax.dynamic_update_index_in_dim(kept_attended, attended, block_index, 0)
        kept_logsum = lax.dynamic_update_index_in_dim(kept_logsum, log_total, block_index, 0)
        kept_input = lax.dynamic_update_index_in_dim(kept_input, layer_input, block_index, 0)
        kept_hidden = lax.dynamic_update_index_in_dim(kept_hidden, hidden, block_index, 0)
        kept_normed_two = lax.dynamic_update_index_in_dim(
            kept_normed_two, normed_two, block_index, 0
        )
        kept_pre = lax.dynamic_update_index_in_dim(kept_pre, pre_active, block_index, 0)
        outputs = lax.dynamic_update_index_in_dim(outputs, result_low, block_index, 0)
        received = from_behind(result_low, "section", 1).astype(f32)
    key_rows = kv_cache[..., :HD]
    value_rows = kv_cache[..., HD:]
    sharded_total = (
        jnp.zeros(w_query.shape, f32),
        jnp.zeros(b_query.shape, f32),
        jnp.zeros(w_out.shape, f32),
        jnp.zeros(w_up.shape, f32),
        jnp.zeros(b_up.shape, f32),
        jnp.zeros(w_down.shape, f32),
    )
    common_total = (
        jnp.zeros(gain_one.shape, f32),
        jnp.zeros(bias_one.shape, f32),
        jnp.zeros(b_out.shape, f32),
        jnp.zeros(gain_two.shape, f32),
        jnp.zeros(bias_two.shape, f32),
        jnp.zeros(b_down.shape, f32),
    )
    pair_total = (jnp.zeros(w_pairs.shape, f32), jnp.zeros((HD,), f32))
    sharded_total = sharded_total + pair_total
    pair_grad_acc = jnp.zeros((total_len, seq_count, 2 * HD), f32)
    input_grads = jnp.zeros((blocks, own_count, seq_count, model_dim), f32)
    received_back = jnp.zeros((own_count, seq_count, model_dim), f32)
    for turn in range(blocks + 1):
        step_count = turn - (1 - section)
        valid = (step_count >= 0) & (step_count < blocks)
        valid_scale = valid.astype(f32)
        block_index = blocks - 1 - jnp.clip(step_count, 0, blocks - 1)
        from_cot = lax.dynamic_index_in_dim(cotangent, block_index, 0, keepdims=False).astype(f32)
        grad_out = jnp.where(section == 1, from_cot, received_back) * valid_scale
        pre_active = lax.dynamic_index_in_dim(kept_pre, block_index, 0, keepdims=False)
        normed_two = lax.dynamic_index_in_dim(kept_normed_two, block_index, 0, keepdims=False)
        active = gelu_tanh(pre_active).astype(bf16)
        grad_mlp = gather_rows(grad_out.astype(bf16))
        grad_active = jnp.einsum("rsd,fd->rsf", grad_mlp, w_down, preferred_element_type=f32)
        gelu_back = jax.vjp(gelu_tanh, pre_active)[1]
        grad_pre = gelu_back(grad_active)[0].astype(bf16)
        down_w_term = jnp.einsum("rsf,rsd->fd", active, grad_mlp, preferred_element_type=f32)
        up_w_term = jnp.einsum("rsd,rsf->df", normed_two, grad_pre, preferred_element_type=f32)
        up_b_term = jnp.sum(grad_pre.astype(f32), axis=(0, 1))
        down_b_term = jnp.sum(grad_out, axis=(0, 1))

        def feed_back_term(start, count, grad_pre=grad_pre):
            return jnp.einsum("rsf,df->rsd", grad_pre, w_up, preferred_element_type=f32)

        grad_normed_two = sum_rows(feed_back_term, own_count)
        hidden_own = lax.dynamic_index_in_dim(kept_hidden, block_index, 0, keepdims=False)
        norm_back_two = jax.vjp(layer_norm, hidden_own, gain_two, bias_two)[1]
        grad_hidden_norm, gain_two_term, bias_two_term = norm_back_two(grad_normed_two)
        grad_hidden = grad_out + grad_hidden_norm
        out_b_term = jnp.sum(grad_hidden, axis=(0, 1))
        grad_branch = gather_rows(grad_hidden.astype(bf16))
        attended = lax.dynamic_index_in_dim(kept_attended, block_index, 0, keepdims=False)
        out_w_term = jnp.einsum("rse,rsd->ed", attended, grad_branch, preferred_element_type=f32)
        grad_attended = jnp.einsum(
            "rsd,ed->rse", grad_branch, w_out, preferred_element_type=f32
        ).astype(bf16)
        grad_attended = grad_attended.reshape(block_len, seq_count, heads_local, HD)
        query = lax.dynamic_index_in_dim(kept_query, block_index, 0, keepdims=False)
        query_heads = query.reshape(block_len, seq_count, heads_local, HD)
        log_total = lax.dynamic_index_in_dim(kept_logsum, block_index, 0, keepdims=False)
        visible = positions < (block_index + 1) * block_len
        scores = (
            jnp.einsum("qshd,ksd->sqhk", query_heads, key_rows, preferred_element_type=f32)
            * score_scale
        )
        scores = jnp.where(visible, scores, -1e30)
        probabilities = jnp.exp(scores - log_total[..., None])
        grad_probs = jnp.einsum(
            "qshd,ksd->sqhk", grad_attended, value_rows, preferred_element_type=f32
        )
        row_inner = jnp.sum(probabilities * grad_probs, axis=-1, keepdims=True)
        grad_scores = (probabilities * (grad_probs - row_inner)).astype(bf16)
        grad_query = (
            jnp.einsum("sqhk,ksd->qshd", grad_scores, key_rows, preferred_element_type=f32)
            * score_scale
        )
        grad_query = grad_query.astype(bf16).reshape(block_len, seq_count, heads_local * HD)
        grad_keys = (
            jnp.einsum("sqhk,qshd->ksd", grad_scores, query_heads, preferred_element_type=f32)
            * score_scale
        )
        grad_values = jnp.einsum(
            "sqhk,qshd->ksd", probabilities.astype(bf16), grad_attended, preferred_element_type=f32
        )
        pair_grad_acc = pair_grad_acc + jnp.concatenate([grad_keys, grad_values], axis=-1)
        block_pairs = lax.dynamic_slice_in_dim(pair_grad_acc, block_index * block_len, block_len, 0)
        grad_pairs = (
            lax.psum(block_pairs.astype(jnp.bfloat16), "tensor").astype(jnp.float32) * valid_scale
        ).astype(bf16)
        normed = lax.dynamic_index_in_dim(kept_normed, block_index, 0, keepdims=False)
        query_w_term = jnp.einsum("rsd,rse->de", normed, grad_query, preferred_element_type=f32)
        query_b_term = jnp.sum(grad_query.astype(f32), axis=(0, 1))
        own_pairs = lax.dynamic_slice_in_dim(grad_pairs, own_start, own_count, 0)
        pair_w_term = jnp.einsum("rsd,rsc->dc", normed, grad_pairs, preferred_element_type=f32)
        value_b_term = jnp.sum(grad_pairs[..., HD:].astype(f32), axis=(0, 1))

        def attention_back_term(start, count, grad_query=grad_query):
            return jnp.einsum("rse,de->rsd", grad_query, w_query, preferred_element_type=f32)

        grad_normed = sum_rows(attention_back_term, own_count)
        grad_normed = grad_normed + jnp.einsum(
            "rsc,dc->rsd", own_pairs, w_pairs, preferred_element_type=f32
        )
        layer_input = lax.dynamic_index_in_dim(kept_input, block_index, 0, keepdims=False)
        norm_back_one = jax.vjp(layer_norm, layer_input, gain_one, bias_one)[1]
        grad_input_norm, gain_one_term, bias_one_term = norm_back_one(grad_normed)
        grad_input = grad_hidden + grad_input_norm
        previous = lax.dynamic_index_in_dim(input_grads, block_index, 0, keepdims=False)
        input_grads = lax.dynamic_update_index_in_dim(
            input_grads, jnp.where(valid, grad_input, previous), block_index, 0
        )
        received_back = from_behind(grad_input.astype(jnp.bfloat16), "section", -1).astype(
            grad_input.dtype
        )
        sharded_terms = (query_w_term, query_b_term, out_w_term, up_w_term, up_b_term, down_w_term)
        common_terms = (
            gain_one_term,
            bias_one_term,
            out_b_term,
            gain_two_term,
            bias_two_term,
            down_b_term,
        )
        pair_terms = (pair_w_term, value_b_term)
        sharded_terms = sharded_terms + pair_terms
        sharded_total = jax.tree.map(jnp.add, sharded_total, sharded_terms)
        common_total = jax.tree.map(jnp.add, common_total, common_terms)
    sharded_total = jax.tree.map(
        lambda part: part.astype(jnp.float32), lax.psum(for_sending(sharded_total), "dp")
    )
    common_total = lax.psum(common_total, ("tensor", "dp"))
    pair_w_grad, value_b_grad = (sharded_total[6], sharded_total[7])
    return (
        outputs[None],
        input_grads[None],
        common_total[0][None],
        common_total[1][None],
        sharded_total[0][None],
        sharded_total[1][None],
        pair_w_grad[None],
        value_b_grad[None],
        sharded_total[2][None],
        common_total[2][None],
        common_total[3][None],
        common_total[4][None],
        sharded_total[3][None],
        sharded_total[4][None],
        sharded_total[5][None],
        common_total[5][None],
    )


def solution(mesh):
    placed = (
        P(None, "tensor", "dp", None),
        P(None, "tensor", "dp", None),
        P("section", None),
        P("section", None),
        P("section", None, "tensor"),
        P("section", "tensor"),
        P("section", None, None),
        P("section", None),
        P("section", "tensor", None),
        P("section", None),
        P("section", None),
        P("section", None),
        P("section", None, "tensor"),
        P("section", "tensor"),
        P("section", "tensor", None),
        P("section", None),
    )
    return jax.shard_map(
        on_device,
        mesh=mesh,
        in_specs=placed,
        out_specs=(
            P("section", None, "tensor", "dp", None),
            P("section", None, "tensor", "dp", None),
            P("section", None),
            P("section", None),
            P("section", None, "tensor"),
            P("section", "tensor"),
            P("section", None, None),
            P("section", None),
            P("section", "tensor", None),
            P("section", None),
            P("section", None),
            P("section", None),
            P("section", None, "tensor"),
            P("section", "tensor"),
            P("section", "tensor", None),
            P("section", None),
        ),
        check_vma=False,
    )
```

profile of v0, /device:TPU:0, one launch (start us, length us, event | category | flops | bytes accessed | tf_op | source)
XLA Modules:
  0.0 2236.9 jit_solution(8627879829273172787)
XLA Ops:
  15.2 29.4 %all-gather.21.cloned.1.call-done = bf16[256,1,2048]{2,0,1:T(8,128)(2,1)} async-done(((bf16[64,1,2048]{2,0,1:T(8,128)(2,1)}), bf16[256,1,2048]{2,0,1:T(8,128)(2,1)}) %all-gather.21.cloned.1.call-update) | async-done | bytes 1048592 | tf_op jit(solution)/shard_map/all_gather | solution.py:32
  53.2 26.7 %reduce-scatter.21.cloned.1.call-done = bf16[64,1,2048]{2,0,1:T(8,128)(2,1)} async-done(((bf16[256,1,2048]{2,0,1:T(8,128)(2,1)}), bf16[64,1,2048]{2,0,1:T(8,128)(2,1)}) %reduce-scatter.21.cloned.1.call-update) | async-done | bytes 262160 | tf_op jit(solution)/shard_map/reduce_scatter | solution.py:36
  85.2 26.6 %all-gather.23.cloned.1.call-done = bf16[256,1,2048]{2,0,1:T(8,128)(2,1)} async-done(((bf16[64,1,2048]{2,0,1:T(8,128)(2,1)}), bf16[256,1,2048]{2,0,1:T(8,128)(2,1)}) %all-gather.23.cloned.1.call-update) | async-done | bytes 1048592 | tf_op jit(solution)/shard_map/all_gather | solution.py:32
  127.1 26.7 %reduce-scatter.23.cloned.1.call-done = bf16[64,1,2048]{2,0,1:T(8,128)(2,1)} async-done(((bf16[256,1,2048]{2,0,1:T(8,128)(2,1)}), bf16[64,1,2048]{2,0,1:T(8,128)(2,1)}) %reduce-scatter.23.cloned.1.call-update) | async-done | bytes 262160 | tf_op jit(solution)/shard_map/reduce_scatter | solution.py:36
  170.1 27.7 %all-gather.25.cloned.1.call-done = bf16[256,1,2048]{2,0,1:T(8,128)(2,1)} async-done(((bf16[64,1,2048]{2,0,1:T(8,128)(2,1)}), bf16[256,1,2048]{2,0,1:T(8,128)(2,1)}) %all-gather.25.cloned.1.call-update) | async-done | bytes 1048592 | tf_op jit(solution)/shard_map/all_gather | solution.py:32
  206.2 26.7 %reduce-scatter.25.cloned.1.call-done = bf16[64,1,2048]{2,0,1:T(8,128)(2,1)} async-done(((bf16[256,1,2048]{2,0,1:T(8,128)(2,1)}), bf16[64,1,2048]{2,0,1:T(8,128)(2,1)}) %reduce-scatter.25.cloned.1.call-update) | async-done | bytes 262160 | tf_op jit(solution)/shard_map/reduce_scatter | solution.py:36
  235.4 26.7 %all-gather.27.cloned.1.call-done = bf16[256,1,2048]{2,0,1:T(8,128)(2,1)} async-done(((bf16[64,1,2048]{2,0,1:T(8,128)(2,1)}), bf16[256,1,2048]{2,0,1:T(8,128)(2,1)}) %all-gather.27.cloned.1.call-update) | async-done | bytes 1048592 | tf_op jit(solution)/shard_map/all_gather | solution.py:32
  276.4 26.8 %reduce-scatter.27.cloned.1.call-done = bf16[64,1,2048]{2,0,1:T(8,128)(2,1)} async-done(((bf16[256,1,2048]{2,0,1:T(8,128)(2,1)}), bf16[64,1,2048]{2,0,1:T(8,128)(2,1)}) %reduce-scatter.27.cloned.1.call-update) | async-done | bytes 262160 | tf_op jit(solution)/shard_map/reduce_scatter | solution.py:36
  319.5 27.4 %all-gather.29.cloned.1.call-done = bf16[256,1,2048]{2,0,1:T(8,128)(2,1)} async-done(((bf16[64,1,2048]{2,0,1:T(8,128)(2,1)}), bf16[256,1,2048]{2,0,1:T(8,128)(2,1)}) %all-gather.29.cloned.1.call-update) | async-done | bytes 1048592 | tf_op jit(solution)/shard_map/all_gather | solution.py:32
  355.9 26.7 %reduce-scatter.29.cloned.1.call-done = bf16[64,1,2048]{2,0,1:T(8,128)(2,1)} async-done(((bf16[256,1,2048]{2,0,1:T(8,128)(2,1)}), bf16[64,1,2048]{2,0,1:T(8,128)(2,1)}) %reduce-scatter.29.cloned.1.call-update) | async-done | bytes 262160 | tf_op jit(solution)/shard_map/reduce_scatter | solution.py:36
  385.7 26.7 %all-gather.31.cloned.1.call-done = bf16[256,1,2048]{2,0,1:T(8,128)(2,1)} async-done(((bf16[64,1,2048]{2,0,1:T(8,128)(2,1)}), bf16[256,1,2048]{2,0,1:T(8,128)(2,1)}) %all-gather.31.cloned.1.call-update) | async-done | bytes 1048592 | tf_op jit(solution)/shard_map/all_gather | solution.py:32
  426.7 26.7 %reduce-scatter.31.cloned.1.call-done = bf16[64,1,2048]{2,0,1:T(8,128)(2,1)} async-done(((bf16[256,1,2048]{2,0,1:T(8,128)(2,1)}), bf16[64,1,2048]{2,0,1:T(8,128)(2,1)}) %reduce-scatter.31.cloned.1.call-update) | async-done | bytes 262160 | tf_op jit(solution)/shard_map/reduce_scatter | solution.py:36
  469.6 27.6 %all-gather.33.cloned.1.call-done = bf16[256,1,2048]{2,0,1:T(8,128)(2,1)} async-done(((bf16[64,1,2048]{2,0,1:T(8,128)(2,1)}), bf16[256,1,2048]{2,0,1:T(8,128)(2,1)}) %all-gather.33.cloned.1.call-update) | async-done | bytes 1048592 | tf_op jit(solution)/shard_map/all_gather | solution.py:32
  506.4 26.7 %reduce-scatter.33.cloned.1.call-done = bf16[64,1,2048]{2,0,1:T(8,128)(2,1)} async-done(((bf16[256,1,2048]{2,0,1:T(8,128)(2,1)}), bf16[64,1,2048]{2,0,1:T(8,128)(2,1)}) %reduce-scatter.33.cloned.1.call-update) | async-done | bytes 262160 | tf_op jit(solution)/shard_map/reduce_scatter | solution.py:36
  536.1 26.7 %all-gather.35.cloned.1.call-done = bf16[256,1,2048]{2,0,1:T(8,128)(2,1)} async-done(((bf16[64,1,2048]{2,0,1:T(8,128)(2,1)}), bf16[256,1,2048]{2,0,1:T(8,128)(2,1)}) %all-gather.35.cloned.1.call-update) | async-done | bytes 1048592 | tf_op jit(solution)/shard_map/all_gather | solution.py:32
  577.1 26.8 %reduce-scatter.35.cloned.1.call-done = bf16[64,1,2048]{2,0,1:T(8,128)(2,1)} async-done(((bf16[256,1,2048]{2,0,1:T(8,128)(2,1)}), bf16[64,1,2048]{2,0,1:T(8,128)(2,1)}) %reduce-scatter.35.cloned.1.call-update) | async-done | bytes 262160 | tf_op jit(solution)/shard_map/reduce_scatter | solution.py:36
  620.0 27.8 %all-gather.37.cloned.1.call-done = bf16[256,1,2048]{2,0,1:T(8,128)(2,1)} async-done(((bf16[64,1,2048]{2,0,1:T(8,128)(2,1)}), bf16[256,1,2048]{2,0,1:T(8,128)(2,1)}) %all-gather.37.cloned.1.call-update) | async-done | bytes 1048592 | tf_op jit(solution)/shard_map/all_gather | solution.py:32
  656.9 26.7 %reduce-scatter.37.cloned.1.call-done = bf16[64,1,2048]{2,0,1:T(8,128)(2,1)} async-done(((bf16[256,1,2048]{2,0,1:T(8,128)(2,1)}), bf16[64,1,2048]{2,0,1:T(8,128)(2,1)}) %reduce-scatter.37.cloned.1.call-update) | async-done | bytes 262160 | tf_op jit(solution)/shard_map/reduce_scatter | solution.py:36
  721.4 20.9 all-gather.41.cloned.1.call-done
  772.6 12.6 reduce-scatter.41.cloned.1.call-done
  804.9 15.0 all-gather.43.cloned.1.call-done
  850.9 16.6 all-reduce.11.cloned.1.call-done
  868.4 28.7 %reduce-scatter.43.cloned.1.call-done = bf16[64,1,2048]{2,0,1:T(8,128)(2,1)} async-done(((bf16[256,1,2048]{2,0,1:T(8,128)(2,1)}), bf16[64,1,2048]{2,0,1:T(8,128)(2,1)}) %reduce-scatter.43.cloned.1.call-update) | async-done | bytes 262160 | tf_op jit(solution)/shard_map/reduce_scatter | solution.py:36
  913.3 26.0 %all-gather.45.cloned.1.call-done = bf16[256,1,2048]{2,0,1:T(8,128)(2,1)} async-done(((bf16[64,1,2048]{2,0,1:T(8,128)(2,1)}), bf16[256,1,2048]{2,0,1:T(8,128)(2,1)}) %all-gather.45.cloned.1.call-update) | async-done | bytes 1048592 | tf_op jit(solution)/shard_map/all_gather | solution.py:32
  956.6 25.6 %reduce-scatter.45.cloned.1.call-done = bf16[64,1,2048]{2,0,1:T(8,128)(2,1)} async-done(((bf16[256,1,2048]{2,0,1:T(8,128)(2,1)}), bf16[64,1,2048]{2,0,1:T(8,128)(2,1)}) %reduce-scatter.45.cloned.1.call-update) | async-done | bytes 262160 | tf_op jit(solution)/shard_map/reduce_scatter | solution.py:36
  995.0 22.0 all-gather.47.cloned.1.call-done
  1045.5 20.9 all-reduce.13.cloned.1.call-done
  1067.9 28.1 %reduce-scatter.47.cloned.1.call-done = bf16[64,1,2048]{2,0,1:T(8,128)(2,1)} async-done(((bf16[256,1,2048]{2,0,1:T(8,128)(2,1)}), bf16[64,1,2048]{2,0,1:T(8,128)(2,1)}) %reduce-scatter.47.cloned.1.call-update) | async-done | bytes 262160 | tf_op jit(solution)/shard_map/reduce_scatter | solution.py:36
  1112.6 25.8 %all-gather.49.cloned.1.call-done = bf16[256,1,2048]{2,0,1:T(8,128)(2,1)} async-done(((bf16[64,1,2048]{2,0,1:T(8,128)(2,1)}), bf16[256,1,2048]{2,0,1:T(8,128)(2,1)}) %all-gather.49.cloned.1.call-update) | async-done | bytes 1048592 | tf_op jit(solution)/shard_map/all_gather | solution.py:32
  1155.6 25.7 %reduce-scatter.49.cloned.1.call-done = bf16[64,1,2048]{2,0,1:T(8,128)(2,1)} async-done(((bf16[256,1,2048]{2,0,1:T(8,128)(2,1)}), bf16[64,1,2048]{2,0,1:T(8,128)(2,1)}) %reduce-scatter.49.cloned.1.call-update) | async-done | bytes 262160 | tf_op jit(solution)/shard_map/reduce_scatter | solution.py:36
  1193.8 22.2 all-gather.51.cloned.1.call-done
  1242.7 22.7 %all-reduce.15.cloned.1.call-done = bf16[256,1,256]{0,2,1:T(8,128)(2,1)} async-done(((bf16[256,1,256]{0,2,1:T(8,128)(2,1)}), bf16[256,1,256]{0,2,1:T(8,128)(2,1)}) %all-reduce.15.cloned.1.call-update) | async-done | bytes 131088 | tf_op jit(solution)/shard_map/psum | solution.py:241
  1266.9 28.2 %reduce-scatter.51.cloned.1.call-done = bf16[64,1,2048]{2,0,1:T(8,128)(2,1)} async-done(((bf16[256,1,2048]{2,0,1:T(8,128)(2,1)}), bf16[64,1,2048]{2,0,1:T(8,128)(2,1)}) %reduce-scatter.51.cloned.1.call-update) | async-done | bytes 262160 | tf_op jit(solution)/shard_map/reduce_scatter | solution.py:36
  1311.7 25.7 %all-gather.53.cloned.1.call-done = bf16[256,1,2048]{2,0,1:T(8,128)(2,1)} async-done(((bf16[64,1,2048]{2,0,1:T(8,128)(2,1)}), bf16[256,1,2048]{2,0,1:T(8,128)(2,1)}) %all-gather.53.cloned.1.call-update) | async-done | bytes 1048592 | tf_op jit(solution)/shard_map/all_gather | solution.py:32
  1354.7 25.6 %reduce-scatter.53.cloned.1.call-done = bf16[64,1,2048]{2,0,1:T(8,128)(2,1)} async-done(((bf16[256,1,2048]{2,0,1:T(8,128)(2,1)}), bf16[64,1,2048]{2,0,1:T(8,128)(2,1)}) %reduce-scatter.53.cloned.1.call-update) | async-done | bytes 262160 | tf_op jit(solution)/shard_map/reduce_scatter | solution.py:36
  1393.8 21.3 all-gather.55.cloned.1.call-done
  1444.5 20.0 all-reduce.17.cloned.1.call-done
  1466.0 28.0 %reduce-scatter.55.cloned.1.call-done = bf16[64,1,2048]{2,0,1:T(8,128)(2,1)} async-done(((bf16[256,1,2048]{2,0,1:T(8,128)(2,1)}), bf16[64,1,2048]{2,0,1:T(8,128)(2,1)}) %reduce-scatter.55.cloned.1.call-update) | async-done | bytes 262160 | tf_op jit(solution)/shard_map/reduce_scatter | solution.py:36
  1516.6 20.5 all-gather.57.cloned.1.call-done
  1561.3 18.7 reduce-scatter.57.cloned.1.call-done
  1600.7 13.6 all-gather.59.cloned.1.call-done
  1745.7 26.9 %fusion.41 = bf16[1,2048,2048]{2,1,0:T(8,128)(2,1)} fusion(f32[2048,2048]{1,0:T(8,128)} %fusion.438, f32[2048,2048]{1,0:T(8,128)} %fusion.440, f32[2048,2048]{1,0:T(8,128)} %fusion.444, f32[2048,2048]{1,0:T(8,128)} %fusion.442, bf16[256,1,2048]{2,0,1:T(8,128)(2,1)S(1)} %copy-done.77, f32[4,256,1,2048]{3,1,2,0:T(8,128)} %get-tuple-element.207, s32[]{:T(128)S(6)} %select_n.364), kind=kOutput, calls=%fused_computation.43 | convolution fusion | flops 2173173760 | bytes 78643200 | tf_op jit(solution)/shard_map/rsf,rsd->fd/dot_general | solution.py:190
  1776.0 27.2 %fusion.40 = bf16[1,2048,2048]{2,1,0:T(8,128)(2,1)} fusion(bf16[256,2048]{1,0:T(8,128)(2,1)} %copy-done.78, f32[2048,2048]{1,0:T(8,128)} %fusion.447, f32[2048,2048]{1,0:T(8,128)} %fusion.449, f32[2048,2048]{1,0:T(8,128)} %fusion.453, f32[2048,2048]{1,0:T(8,128)} %fusion.451, bf16[4,256,1,2048]{3,1,2,0:T(8,128)(2,1)} %bitcast_dynamic-update-slice_fusion.5, ...), kind=kOutput, calls=%fused_computation.42 | convolution fusion | flops 2168455168 | bytes 77594624 | tf_op jit(solution)/shard_map/rsd,rsf->df/dot_general | solution.py:191
  1834.4 11.7 all-reduce.2
  1850.6 61.3 %all-reduce.1 = (f32[1,2048]{1,0:T(1,128)}, f32[1,2048]{1,0:T(1,128)}, f32[1,2048]{1,0:T(1,128)}, f32[1,2048]{1,0:T(1,128)}, f32[1,2048]{1,0:T(1,128)}, /*index=5*/f32[1,2048]{1,0:T(1,128)}) all-reduce(f32[1,2048]{1,0:T(1,128)S(1)} %bitcast.1391, ...), channel_id=1, replica_groups=mesh['section'=2,'tensor'=4,'dp'=4] {'tensor','dp'}, use_global_device_ids=true, to_apply=%region_105.106 | all-reduce | flops 12288 | bytes 98304 | tf_op jit(solution)/shard_map/psum | solution.py:284
  1916.2 281.2 %all-reduce.21.cloned.1.call-done = (bf16[1,2048,512]{2,1,0:T(8,128)(2,1)}, bf16[1,2048,256]{2,1,0:T(8,128)(2,1)}, bf16[1,512,2048]{2,1,0:T(8,128)(2,1)}, bf16[1...) async-done(((bf16[1,2048,512]{2,1,0:T(8,128)(2,1)}, bf16[1,2048,256]{2,1,0:T(8,128)(2,1)}, bf16[1,512,2048]{2,1,0:T(8,128)(2,1)}, bf16[1,2048,2048]{2,1,0:T(8,128)(2,1)}, ...) | async-done | bytes 22020112 | tf_op jit(solution)/shard_map/psum | solution.py:282
  2206.6 11.7 broadcast_in_dim.547
  2218.2 11.7 broadcast_in_dim.551
  (913 shorter events, 786.4 us)
Async XLA Ops:
  7.2 37.4 %all-gather.21.cloned.1.call-start = ((), (), s32[]{:S(2)}) async-start(), calls=%async_computation.20 | async-start | bytes 1310720 | tf_op jit(solution)/shard_map/all_gather | solution.py:32
  13.8 66.1 %reduce-scatter.21.cloned.1.call-start = ((), (), s32[]{:S(2)}) async-start(), calls=%async_computation.21 | async-start | bytes 1310720 | tf_op jit(solution)/shard_map/reduce_scatter | solution.py:36
  53.1 58.8 %all-gather.23.cloned.1.call-start = ((), (), s32[]{:S(2)}) async-start(), calls=%async_computation.22 | async-start | bytes 1310720 | tf_op jit(solution)/shard_map/all_gather | solution.py:32
  85.1 68.7 %reduce-scatter.23.cloned.1.call-start = ((), (), s32[]{:S(2)}) async-start(), calls=%async_computation.23 | async-start | bytes 1310720 | tf_op jit(solution)/shard_map/reduce_scatter | solution.py:36
  127.1 70.7 %all-gather.25.cloned.1.call-start = ((), (), s32[]{:S(2)}) async-start(), calls=%async_computation.24 | async-start | bytes 1310720 | tf_op jit(solution)/shard_map/all_gather | solution.py:32
  169.8 63.1 %reduce-scatter.25.cloned.1.call-start = ((), (), s32[]{:S(2)}) async-start(), calls=%async_computation.25 | async-start | bytes 1310720 | tf_op jit(solution)/shard_map/reduce_scatter | solution.py:36
  206.2 55.9 %all-gather.27.cloned.1.call-start = ((), (), s32[]{:S(2)}) async-start(), calls=%async_computation.26 | async-start | bytes 1310720 | tf_op jit(solution)/shard_map/all_gather | solution.py:32
  235.3 67.8 %reduce-scatter.27.cloned.1.call-start = ((), (), s32[]{:S(2)}) async-start(), calls=%async_computation.27 | async-start | bytes 1310720 | tf_op jit(solution)/shard_map/reduce_scatter | solution.py:36
  276.4 70.5 %all-gather.29.cloned.1.call-start = ((), (), s32[]{:S(2)}) async-start(), calls=%async_computation.28 | async-start | bytes 1310720 | tf_op jit(solution)/shard_map/all_gather | solution.py:32
  319.0 63.7 %reduce-scatter.29.cloned.1.call-start = ((), (), s32[]{:S(2)}) async-start(), calls=%async_computation.29 | async-start | bytes 1310720 | tf_op jit(solution)/shard_map/reduce_scatter | solution.py:36
  355.9 56.5 %all-gather.31.cloned.1.call-start = ((), (), s32[]{:S(2)}) async-start(), calls=%async_computation.30 | async-start | bytes 1310720 | tf_op jit(solution)/shard_map/all_gather | solution.py:32
  385.6 67.8 %reduce-scatter.31.cloned.1.call-start = ((), (), s32[]{:S(2)}) async-start(), calls=%async_computation.31 | async-start | bytes 1310720 | tf_op jit(solution)/shard_map/reduce_scatter | solution.py:36
  426.7 70.6 %all-gather.33.cloned.1.call-start = ((), (), s32[]{:S(2)}) async-start(), calls=%async_computation.32 | async-start | bytes 1310720 | tf_op jit(solution)/shard_map/all_gather | solution.py:32
  469.4 63.7 %reduce-scatter.33.cloned.1.call-start = ((), (), s32[]{:S(2)}) async-start(), calls=%async_computation.33 | async-start | bytes 1310720 | tf_op jit(solution)/shard_map/reduce_scatter | solution.py:36
  506.3 56.5 %all-gather.35.cloned.1.call-start = ((), (), s32[]{:S(2)}) async-start(), calls=%async_computation.34 | async-start | bytes 1310720 | tf_op jit(solution)/shard_map/all_gather | solution.py:32
  536.1 67.9 %reduce-scatter.35.cloned.1.call-start = ((), (), s32[]{:S(2)}) async-start(), calls=%async_computation.35 | async-start | bytes 1310720 | tf_op jit(solution)/shard_map/reduce_scatter | solution.py:36
  577.1 70.7 %all-gather.37.cloned.1.call-start = ((), (), s32[]{:S(2)}) async-start(), calls=%async_computation.36 | async-start | bytes 1310720 | tf_op jit(solution)/shard_map/all_gather | solution.py:32
  619.9 63.7 %reduce-scatter.37.cloned.1.call-start = ((), (), s32[]{:S(2)}) async-start(), calls=%async_computation.37 | async-start | bytes 1310720 | tf_op jit(solution)/shard_map/reduce_scatter | solution.py:36
  656.9 56.5 %all-gather.39.cloned.1.call-start = ((), (), s32[]{:S(2)}) async-start(), calls=%async_computation.38 | async-start | bytes 1310720 | tf_op jit(solution)/shard_map/all_gather | solution.py:32
  686.6 55.7 %all-gather.41.cloned.1.call-start = ((), (), s32[]{:S(2)}) async-start(), calls=%async_computation.40 | async-start | bytes 1310720 | tf_op jit(solution)/shard_map/all_gather | solution.py:32
  689.0 96.1 %reduce-scatter.41.cloned.1.call-start = ((), (), s32[]{:S(2)}) async-start(), calls=%async_computation.41 | async-start | bytes 1310720 | tf_op jit(solution)/shard_map/reduce_scatter | solution.py:36
  758.3 61.6 %all-gather.43.cloned.1.call-start = ((), (), s32[]{:S(2)}) async-start(), calls=%async_computation.42 | async-start | bytes 1310720 | tf_op jit(solution)/shard_map/all_gather | solution.py:32
  793.1 74.4 %all-reduce.11.cloned.1.call-start = ((), (), s32[]{:S(2)}) async-start(), calls=%async_computation.44 | async-start | bytes 262144 | tf_op jit(solution)/shard_map/psum | solution.py:241
  833.4 63.7 %reduce-scatter.43.cloned.1.call-start = ((), (), s32[]{:S(2)}) async-start(), calls=%async_computation.43 | async-start | bytes 1310720 | tf_op jit(solution)/shard_map/reduce_scatter | solution.py:36
  836.8 102.5 %all-gather.45.cloned.1.call-start = ((), (), s32[]{:S(2)}) async-start(), calls=%async_computation.45 | async-start | bytes 1310720 | tf_op jit(solution)/shard_map/all_gather | solution.py:32
  901.4 10.1 collective-permute-start.4
  913.3 68.9 %reduce-scatter.45.cloned.1.call-start = ((), (), s32[]{:S(2)}) async-start(), calls=%async_computation.46 | async-start | bytes 1310720 | tf_op jit(solution)/shard_map/reduce_scatter | solution.py:36
  955.4 61.6 %all-gather.47.cloned.1.call-start = ((), (), s32[]{:S(2)}) async-start(), calls=%async_computation.47 | async-start | bytes 1310720 | tf_op jit(solution)/shard_map/all_gather | solution.py:32
  990.3 76.1 %all-reduce.13.cloned.1.call-start = ((), (), s32[]{:S(2)}) async-start(), calls=%async_computation.49 | async-start | bytes 262144 | tf_op jit(solution)/shard_map/psum | solution.py:241
  1032.3 63.8 %reduce-scatter.47.cloned.1.call-start = ((), (), s32[]{:S(2)}) async-start(), calls=%async_computation.48 | async-start | bytes 1310720 | tf_op jit(solution)/shard_map/reduce_scatter | solution.py:36
  1035.7 102.6 %all-gather.49.cloned.1.call-start = ((), (), s32[]{:S(2)}) async-start(), calls=%async_computation.50 | async-start | bytes 1310720 | tf_op jit(solution)/shard_map/all_gather | solution.py:32
  1100.4 10.1 collective-permute-start.5
  1112.3 68.9 %reduce-scatter.49.cloned.1.call-start = ((), (), s32[]{:S(2)}) async-start(), calls=%async_computation.51 | async-start | bytes 1310720 | tf_op jit(solution)/shard_map/reduce_scatter | solution.py:36
  1154.4 61.6 %all-gather.51.cloned.1.call-start = ((), (), s32[]{:S(2)}) async-start(), calls=%async_computation.52 | async-start | bytes 1310720 | tf_op jit(solution)/shard_map/all_gather | solution.py:32
  1189.3 76.1 %all-reduce.15.cloned.1.call-start = ((), (), s32[]{:S(2)}) async-start(), calls=%async_computation.54 | async-start | bytes 262144 | tf_op jit(solution)/shard_map/psum | solution.py:241
  1231.2 63.9 %reduce-scatter.51.cloned.1.call-start = ((), (), s32[]{:S(2)}) async-start(), calls=%async_computation.53 | async-start | bytes 1310720 | tf_op jit(solution)/shard_map/reduce_scatter | solution.py:36
  1234.7 102.7 %all-gather.53.cloned.1.call-start = ((), (), s32[]{:S(2)}) async-start(), calls=%async_computation.55 | async-start | bytes 1310720 | tf_op jit(solution)/shard_map/all_gather | solution.py:32
  1311.4 68.9 %reduce-scatter.53.cloned.1.call-start = ((), (), s32[]{:S(2)}) async-start(), calls=%async_computation.56 | async-start | bytes 1310720 | tf_op jit(solution)/shard_map/reduce_scatter | solution.py:36
  1353.5 61.6 %all-gather.55.cloned.1.call-start = ((), (), s32[]{:S(2)}) async-start(), calls=%async_computation.57 | async-start | bytes 1310720 | tf_op jit(solution)/shard_map/all_gather | solution.py:32
  1388.4 76.1 %all-reduce.17.cloned.1.call-start = ((), (), s32[]{:S(2)}) async-start(), calls=%async_computation.59 | async-start | bytes 262144 | tf_op jit(solution)/shard_map/psum | solution.py:241
  1430.4 63.6 %reduce-scatter.55.cloned.1.call-start = ((), (), s32[]{:S(2)}) async-start(), calls=%async_computation.58 | async-start | bytes 1310720 | tf_op jit(solution)/shard_map/reduce_scatter | solution.py:36
  1433.9 103.2 %all-gather.57.cloned.1.call-start = ((), (), s32[]{:S(2)}) async-start(), calls=%async_computation.60 | async-start | bytes 1310720 | tf_op jit(solution)/shard_map/all_gather | solution.py:32
  1511.1 68.9 %reduce-scatter.57.cloned.1.call-start = ((), (), s32[]{:S(2)}) async-start(), calls=%async_computation.61 | async-start | bytes 1310720 | tf_op jit(solution)/shard_map/reduce_scatter | solution.py:36
  1553.2 61.2 %all-gather.59.cloned.1.call-start = ((), (), s32[]{:S(2)}) async-start(), calls=%async_computation.62 | async-start | bytes 1310720 | tf_op jit(solution)/shard_map/all_gather | solution.py:32
  1587.6 228.8 %all-reduce.19.cloned.1.call-start = ((), (), s32[]{:S(2)}) async-start(), calls=%async_computation.64 | async-start | bytes 262144 | tf_op jit(solution)/shard_map/psum | solution.py:241
  1626.3 198.8 %reduce-scatter.39.cloned.1.call-start = ((), (), s32[]{:S(2)}) async-start(), calls=%async_computation.39 | async-start | bytes 1310720 | tf_op jit(solution)/shard_map/reduce_scatter | solution.py:36
  1636.0 211.8 %reduce-scatter.59.cloned.1.call-start = ((), (), s32[]{:S(2)}) async-start(), calls=%async_computation.63 | async-start | bytes 1310720 | tf_op jit(solution)/shard_map/reduce_scatter | solution.py:36
  1776.0 421.4 %all-reduce.21.cloned.1.call-start = ((), (), s32[]{:S(2)}) async-start(), calls=%async_computation.65 | async-start | bytes 44040192 | tf_op jit(solution)/shard_map/psum | solution.py:282
  (221 other events, 3513.3 us)
Sparse Core Ops, SparseCore 0:
  13.9 30.6 all-gather.20
  53.2 26.6 reduce-scatter.20
  85.3 26.5 all-gather.22
  127.2 26.6 reduce-scatter.22
  169.9 27.7 all-gather.24
  206.3 26.6 reduce-scatter.24
  235.5 26.5 all-gather.26
  276.5 26.6 reduce-scatter.26
  319.1 27.6 all-gather.28
  356.0 26.6 reduce-scatter.28
  385.8 26.5 all-gather.30
  426.8 26.5 reduce-scatter.30
  469.5 27.6 all-gather.32
  506.5 26.6 reduce-scatter.32
  536.2 26.5 all-gather.34
  577.2 26.6 reduce-scatter.34
  620.1 27.6 all-gather.36
  657.0 26.6 reduce-scatter.36
  686.7 26.5 all-gather.38
  714.8 27.4 all-gather.40
  758.5 26.6 reduce-scatter.40
  793.3 26.5 all-gather.42
  833.5 33.9 all-reduce.10
  870.3 26.7 reduce-scatter.42
  913.4 25.8 all-gather.44
  955.5 26.6 reduce-scatter.44
  990.4 26.5 all-gather.46
  1032.4 33.9 all-reduce.12
  1069.2 26.7 reduce-scatter.46
  1112.5 25.8 all-gather.48
  1154.5 26.6 reduce-scatter.48
  1189.4 26.5 all-gather.50
  1231.4 33.9 all-reduce.14
  1268.3 26.7 reduce-scatter.50
  1311.6 25.8 all-gather.52
  1353.6 26.6 reduce-scatter.52
  1388.5 26.5 all-gather.54
  1430.5 33.9 all-reduce.16
  1467.2 26.7 reduce-scatter.54
  1511.2 25.8 all-gather.56
  1553.3 26.6 reduce-scatter.56
  1587.7 26.5 all-gather.58
  1626.4 33.9 all-reduce.18
  1662.7 26.7 reduce-scatter.38
  1776.1 26.6 reduce-scatter.58
  1821.6 375.7 all-reduce.20
where the time goes:
time: 2250 us; the launch traced here: 2240 us
  waiting for transfers between devices  1340 us (60%)
  matrix products  463 us (21%)
  other arithmetic  188 us (8%)
  local copies, waits for them, and re-layouts  126 us (6%)
  blocking collectives  73 us (3%)
  starting transfers between devices  24.6 us (1%)
    all_gather x20, waiting for transfers between devices, gather_rows(): return lax.all_gather(own_rows, 'tensor', axis=0, tiled=True)  468 us
    reduce_scatter x20, waiting for transfers between devices, sum_rows(): lax.psum_scatter(term_fn(jnp.int32(0), own_count * lax.axis_size('tensor'...  462 us
    psum x1, waiting for transfers between devices, on_device(): lax.psum(for_sending(sharded_total), 'dp')  281 us
    psum x5, waiting for transfers between devices, on_device(): lax.psum(block_pairs.astype(jnp.bfloat16), 'tensor').astype(jnp.float32)  80.1 us
    dot_general x5, matrix products, on_device(): jnp.einsum('rsf,rsd->fd', active, grad_mlp, preferred_element_type=f32)  67.2 us
    dot_general x5, matrix products, on_device(): jnp.einsum('rsd,rsf->df', normed_two, grad_pre, preferred_element_type=f32)  66.3 us
    psum x1, blocking collectives, on_device(): common_total = lax.psum(common_total, ('tensor', 'dp'))  61.3 us
    ppermute x8, waiting for transfers between devices, from_behind(): return lax.ppermute(block, axis, route)  52.9 us
  transfers between devices with their start and end apart: 54, of which 51 were waited for; matrix products, arithmetic and copies ran while one was open for 16% of the time, Pallas kernels for 0%

commit v1 on v0

--- a/solution.py
+++ b/solution.py
@@ -7,6 +7,24 @@
 HD = 128
 
 
+def ring_gather(value, axis, dim):
+    ways, here, step = (lax.axis_size(axis), lax.axis_index(axis), value.shape[dim])
+    shape = [n * ways if d == dim else n for d, n in enumerate(value.shape)]
+    full = lax.dynamic_update_slice_in_dim(
+        jnp.zeros(shape, value.dtype), value, here * step, axis=dim
+    )
+    going_up = going_down = value
+    for far in range(1, ways // 2 + 1):
+        going_up = lax.ppermute(going_up, axis, [(d, (d + 1) % ways) for d in range(ways)])
+        full = lax.dynamic_update_slice_in_dim(full, going_up, (here - far) % ways * step, axis=dim)
+        if 2 * far < ways:
+            going_down = lax.ppermute(going_down, axis, [(d, (d - 1) % ways) for d in range(ways)])
+            full = lax.dynamic_update_slice_in_dim(
+                full, going_down, (here + far) % ways * step, axis=dim
+            )
+    return full
+
+
 def from_behind(block, axis, distance):
     devices = range(lax.axis_size(axis))
     route = [(i - distance, i) for i in devices if i - distance in devices]
@@ -29,7 +47,7 @@
 
 
 def gather_rows(own_rows):
-    return lax.all_gather(own_rows, "tensor", axis=0, tiled=True)
+    return ring_gather(own_rows, "tensor", 0)
 
 
 def sum_rows(term_fn, own_count):

time: 2250 us -> 2070 us (0.920)
  waiting for transfers between devices: 1340 us -> 1090 us
  starting transfers between devices: 24.6 us -> 104 us
  local copies, waits for them, and re-layouts: 126 us -> 155 us
  matrix products: 463 us -> 439 us
    all_gather x20 -> x0, waiting for transfers between devices: 468 us -> none  [gather_rows(): return lax.all_gather(own_rows, 'tensor', axis=0, tiled=True)]
    ppermute x0 -> x60, waiting for transfers between devices: none -> 297 us  [the longest x40 233 us: ring_gather(): lax.ppermute(going_up, axis, [(d, (d + 1) % ways) for d in range(ways)])]
    ppermute x0 -> x60, starting transfers between devices: none -> 82.6 us  [the longest x20 74.4 us: ring_gather(): lax.ppermute(going_down, axis, [(d, (d - 1) % ways) for d in range(ways)])]
    reduce_scatter x20, waiting for transfers between devices: 462 us -> 392 us  [sum_rows(): lax.psum_scatter(term_fn(jnp.int32(0), own_count * lax.axis_size('tensor'...]
    convert_element_type x18 -> x0, other arithmetic: 23.6 us -> none  [the longest x5 9.11 us: on_device(): layer_norm(layer_input, gain_one, bias_one).astype(bf16)]
  transfers between devices with their start and end apart: 54 -> 94, of which waited for: 51 -> 90; matrix products, arithmetic and copies ran while one was open for 16% -> 18% of each run, Pallas kernels for 0% -> 0%
where the time goes in v1:
time: 2070 us; the launch traced here: 2060 us
  waiting for transfers between devices  1090 us (53%)
  matrix products  439 us (21%)
  other arithmetic  177 us (9%)
  local copies, waits for them, and re-layouts  155 us (7%)
  starting transfers between devices  104 us (5%)
  blocking collectives  71.4 us (3%)
    reduce_scatter x20, waiting for transfers between devices, sum_rows(): lax.psum_scatter(term_fn(jnp.int32(0), own_count * lax.axis_size('tensor'...  392 us
    psum x1, waiting for transfers between devices, on_device(): lax.psum(for_sending(sharded_total), 'dp')  281 us
    ppermute x40, waiting for transfers between devices, ring_gather(): lax.ppermute(going_up, axis, [(d, (d + 1) % ways) for d in range(ways)])  233 us
    psum x5, waiting for transfers between devices, on_device(): lax.psum(block_pairs.astype(jnp.bfloat16), 'tensor').astype(jnp.float32)  76 us
    ppermute x20, starting transfers between devices, ring_gather(): lax.ppermute(going_down, axis, [(d, (d - 1) % ways) for d in range(ways)])  74.4 us
    dot_general x5, matrix products, on_device(): jnp.einsum('rsf,rsd->fd', active, grad_mlp, preferred_element_type=f32)  67.6 us
    dot_general x5, matrix products, on_device(): jnp.einsum('rsd,rsf->df', normed_two, grad_pre, preferred_element_type=f32)  66.3 us
    ppermute x20, waiting for transfers between devices, ring_gather(): lax.ppermute(going_down, axis, [(d, (d - 1) % ways) for d in range(ways)])  64.3 us
  transfers between devices with their start and end apart: 94, of which 90 were waited for; matrix products, arithmetic and copies ran while one was open for 18% of the time, Pallas kernels for 0%

profile of v1, /device:TPU:0, one launch (start us, length us, event | category | flops | bytes accessed | tf_op | source)
XLA Modules:
  0.0 2059.7 jit_solution(6091803770521869871)
XLA Ops:
  47.3 26.5 %reduce-scatter.21.cloned.1.call-done = bf16[64,1,2048]{2,0,1:T(8,128)(2,1)} async-done(((bf16[256,1,2048]{2,0,1:T(8,128)(2,1)}), bf16[64,1,2048]{2,0,1:T(8,128)(2,1)}) %reduce-scatter.21.cloned.1.call-update) | async-done | bytes 262160 | tf_op jit(solution)/shard_map/reduce_scatter | solution.py:54
  114.9 25.3 %reduce-scatter.23.cloned.1.call-done = bf16[64,1,2048]{2,0,1:T(8,128)(2,1)} async-done(((bf16[256,1,2048]{2,0,1:T(8,128)(2,1)}), bf16[64,1,2048]{2,0,1:T(8,128)(2,1)}) %reduce-scatter.23.cloned.1.call-update) | async-done | bytes 262160 | tf_op jit(solution)/shard_map/reduce_scatter | solution.py:54
  188.0 26.4 %reduce-scatter.25.cloned.1.call-done = bf16[64,1,2048]{2,0,1:T(8,128)(2,1)} async-done(((bf16[256,1,2048]{2,0,1:T(8,128)(2,1)}), bf16[64,1,2048]{2,0,1:T(8,128)(2,1)}) %reduce-scatter.25.cloned.1.call-update) | async-done | bytes 262160 | tf_op jit(solution)/shard_map/reduce_scatter | solution.py:54
  237.3 7.5 bitcast_dynamic-update-slice_fusion.3
  248.4 25.4 %reduce-scatter.27.cloned.1.call-done = bf16[64,1,2048]{2,0,1:T(8,128)(2,1)} async-done(((bf16[256,1,2048]{2,0,1:T(8,128)(2,1)}), bf16[64,1,2048]{2,0,1:T(8,128)(2,1)}) %reduce-scatter.27.cloned.1.call-update) | async-done | bytes 262160 | tf_op jit(solution)/shard_map/reduce_scatter | solution.py:54
  294.6 7.5 collective-permute-done.14
  322.1 26.3 %reduce-scatter.29.cloned.1.call-done = bf16[64,1,2048]{2,0,1:T(8,128)(2,1)} async-done(((bf16[256,1,2048]{2,0,1:T(8,128)(2,1)}), bf16[64,1,2048]{2,0,1:T(8,128)(2,1)}) %reduce-scatter.29.cloned.1.call-update) | async-done | bytes 262160 | tf_op jit(solution)/shard_map/reduce_scatter | solution.py:54
  371.3 7.5 bitcast_dynamic-update-slice_fusion.2
  382.4 25.4 %reduce-scatter.31.cloned.1.call-done = bf16[64,1,2048]{2,0,1:T(8,128)(2,1)} async-done(((bf16[256,1,2048]{2,0,1:T(8,128)(2,1)}), bf16[64,1,2048]{2,0,1:T(8,128)(2,1)}) %reduce-scatter.31.cloned.1.call-update) | async-done | bytes 262160 | tf_op jit(solution)/shard_map/reduce_scatter | solution.py:54
  428.8 7.5 collective-permute-done.21
  456.4 26.3 %reduce-scatter.33.cloned.1.call-done = bf16[64,1,2048]{2,0,1:T(8,128)(2,1)} async-done(((bf16[256,1,2048]{2,0,1:T(8,128)(2,1)}), bf16[64,1,2048]{2,0,1:T(8,128)(2,1)}) %reduce-scatter.33.cloned.1.call-update) | async-done | bytes 262160 | tf_op jit(solution)/shard_map/reduce_scatter | solution.py:54
  505.6 7.5 bitcast_dynamic-update-slice_fusion.1
  546.4 9.8 reduce-scatter.35.cloned.1.call-done
  610.9 14.3 reduce-scatter.37.cloned.1.call-done
  651.0 8.1 bitcast_dynamic-update-slice_fusion
  659.0 8.4 convert_reduce_fusion.4
  690.7 9.9 reduce-scatter.41.cloned.1.call-done
  760.6 15.3 all-reduce.11.cloned.1.call-done
  776.8 28.7 %reduce-scatter.43.cloned.1.call-done = bf16[64,1,2048]{2,0,1:T(8,128)(2,1)} async-done(((bf16[256,1,2048]{2,0,1:T(8,128)(2,1)}), bf16[64,1,2048]{2,0,1:T(8,128)(2,1)}) %reduce-scatter.43.cloned.1.call-update) | async-done | bytes 262160 | tf_op jit(solution)/shard_map/reduce_scatter | solution.py:54
  811.0 8.8 collective-permute-done.40
  841.2 8.5 convert_reduce_fusion.3
  859.2 22.9 %reduce-scatter.45.cloned.1.call-done = bf16[64,1,2048]{2,0,1:T(8,128)(2,1)} async-done(((bf16[256,1,2048]{2,0,1:T(8,128)(2,1)}), bf16[64,1,2048]{2,0,1:T(8,128)(2,1)}) %reduce-scatter.45.cloned.1.call-update) | async-done | bytes 262160 | tf_op jit(solution)/shard_map/reduce_scatter | solution.py:54
  938.5 19.8 all-reduce.13.cloned.1.call-done
  959.9 27.9 %reduce-scatter.47.cloned.1.call-done = bf16[64,1,2048]{2,0,1:T(8,128)(2,1)} async-done(((bf16[256,1,2048]{2,0,1:T(8,128)(2,1)}), bf16[64,1,2048]{2,0,1:T(8,128)(2,1)}) %reduce-scatter.47.cloned.1.call-update) | async-done | bytes 262160 | tf_op jit(solution)/shard_map/reduce_scatter | solution.py:54
  993.5 8.8 collective-permute-done.47
  1023.7 8.6 convert_reduce_fusion.2
  1041.8 22.7 %reduce-scatter.49.cloned.1.call-done = bf16[64,1,2048]{2,0,1:T(8,128)(2,1)} async-done(((bf16[256,1,2048]{2,0,1:T(8,128)(2,1)}), bf16[64,1,2048]{2,0,1:T(8,128)(2,1)}) %reduce-scatter.49.cloned.1.call-update) | async-done | bytes 262160 | tf_op jit(solution)/shard_map/reduce_scatter | solution.py:54
  1120.7 20.1 all-reduce.15.cloned.1.call-done
  1142.4 28.1 %reduce-scatter.51.cloned.1.call-done = bf16[64,1,2048]{2,0,1:T(8,128)(2,1)} async-done(((bf16[256,1,2048]{2,0,1:T(8,128)(2,1)}), bf16[64,1,2048]{2,0,1:T(8,128)(2,1)}) %reduce-scatter.51.cloned.1.call-update) | async-done | bytes 262160 | tf_op jit(solution)/shard_map/reduce_scatter | solution.py:54
  1225.4 15.8 reduce-scatter.53.cloned.1.call-done
  1296.7 20.8 %all-reduce.17.cloned.1.call-done = bf16[256,1,256]{0,2,1:T(8,128)(2,1)} async-done(((bf16[256,1,256]{0,2,1:T(8,128)(2,1)}), bf16[256,1,256]{0,2,1:T(8,128)(2,1)}) %all-reduce.17.cloned.1.call-update) | async-done | bytes 131088 | tf_op jit(solution)/shard_map/psum | solution.py:259
  1319.0 28.1 %reduce-scatter.55.cloned.1.call-done = bf16[64,1,2048]{2,0,1:T(8,128)(2,1)} async-done(((bf16[256,1,2048]{2,0,1:T(8,128)(2,1)}), bf16[64,1,2048]{2,0,1:T(8,128)(2,1)}) %reduce-scatter.55.cloned.1.call-update) | async-done | bytes 262160 | tf_op jit(solution)/shard_map/reduce_scatter | solution.py:54
  1383.0 8.6 convert_reduce_fusion
  1400.9 10.4 fusion.447
  1460.2 9.7 fusion.456
  1479.7 9.5 fusion.454
  1489.3 10.0 fusion.445
  1508.9 9.9 fusion.452
  1518.8 10.4 fusion.443
  1538.8 9.9 fusion.450
  1548.7 10.1 fusion.441
  1569.9 26.7 %fusion = bf16[1,2048,2048]{2,1,0:T(8,128)(2,1)} fusion(f32[2048,2048]{1,0:T(8,128)} %fusion.441, f32[2048,2048]{1,0:T(8,128)} %fusion.443, f32[2048,2048]{1,0:T(8,128)} %fusion.447, f32[2048,2048]{1,0:T(8,128)} %fusion.445, bf16[256,2048]{1,0:T(8,128)(2,1)S(1)} %copy-done.55, f32[4,256,1,2048]{3,1,2,0:T(8,128)} %get-tuple-element.244, s32[]{:T(128)S(6)} %select_n.587), kind=kOutput, calls=%fused_computation.2 | convolution fusion | flops 2173173760 | bytes 78643200 | tf_op jit(solution)/shard_map/rsf,rsd->fd/dot_general | solution.py:208
  1600.4 27.3 %fusion.41 = bf16[1,2048,2048]{2,1,0:T(8,128)(2,1)} fusion(bf16[256,2048]{1,0:T(8,128)(2,1)} %copy-done.122, f32[2048,2048]{1,0:T(8,128)} %fusion.450, f32[2048,2048]{1,0:T(8,128)} %fusion.452, f32[2048,2048]{1,0:T(8,128)} %fusion.456, f32[2048,2048]{1,0:T(8,128)} %fusion.454, bf16[4,256,1,2048]{3,1,2,0:T(8,128)(2,1)} %bitcast_dynamic-update-slice_fusion.5, ...), kind=kOutput, calls=%fused_computation.43 | convolution fusion | flops 2168455168 | bytes 77594624 | tf_op jit(solution)/shard_map/rsd,rsf->df/dot_general | solution.py:209
  1659.7 11.2 all-reduce.2
  1675.3 60.3 %all-reduce.1 = (f32[1,2048]{1,0:T(1,128)}, f32[1,2048]{1,0:T(1,128)}, f32[1,2048]{1,0:T(1,128)}, f32[1,2048]{1,0:T(1,128)}, f32[1,2048]{1,0:T(1,128)}, /*index=5*/f32[1,2048]{1,0:T(1,128)}) all-reduce(f32[1,2048]{1,0:T(1,128)S(1)} %bitcast.1447, ...), channel_id=1, replica_groups=mesh['section'=2,'tensor'=4,'dp'=4] {'tensor','dp'}, use_global_device_ids=true, to_apply=%region_105.106 | all-reduce | flops 12288 | bytes 98304 | tf_op jit(solution)/shard_map/psum | solution.py:302
  1739.9 280.6 %all-reduce.21.cloned.1.call-done = (bf16[1,2048,512]{2,1,0:T(8,128)(2,1)}, bf16[1,2048,256]{2,1,0:T(8,128)(2,1)}, bf16[1,512,2048]{2,1,0:T(8,128)(2,1)}, bf16[1...) async-done(((bf16[1,2048,512]{2,1,0:T(8,128)(2,1)}, bf16[1,2048,256]{2,1,0:T(8,128)(2,1)}, bf16[1,512,2048]{2,1,0:T(8,128)(2,1)}, bf16[1,2048,2048]{2,1,0:T(8,128)(2,1)}, ...) | async-done | bytes 22020112 | tf_op jit(solution)/shard_map/psum | solution.py:300
  2029.6 11.7 broadcast_in_dim.547
  2041.3 11.7 broadcast_in_dim.551
  (1129 shorter events, 969.5 us)
Async XLA Ops:
  7.2 66.5 %reduce-scatter.21.cloned.1.call-start = ((), (), s32[]{:S(2)}) async-start(), calls=%async_computation.20 | async-start | bytes 1310720 | tf_op jit(solution)/shard_map/reduce_scatter | solution.py:54
  16.9 13.9 collective-permute-start.1
  47.1 93.1 %reduce-scatter.23.cloned.1.call-start = ((), (), s32[]{:S(2)}) async-start(), calls=%async_computation.21 | async-start | bytes 1310720 | tf_op jit(solution)/shard_map/reduce_scatter | solution.py:54
  78.5 13.6 collective-permute-start.4
  114.8 99.6 %reduce-scatter.25.cloned.1.call-start = ((), (), s32[]{:S(2)}) async-start(), calls=%async_computation.22 | async-start | bytes 1310720 | tf_op jit(solution)/shard_map/reduce_scatter | solution.py:54
  157.3 13.3 collective-permute-start.8
  188.0 85.8 %reduce-scatter.27.cloned.1.call-start = ((), (), s32[]{:S(2)}) async-start(), calls=%async_computation.23 | async-start | bytes 1310720 | tf_op jit(solution)/shard_map/reduce_scatter | solution.py:54
  216.3 13.5 collective-permute-start.11
  248.3 100.2 %reduce-scatter.29.cloned.1.call-start = ((), (), s32[]{:S(2)}) async-start(), calls=%async_computation.24 | async-start | bytes 1310720 | tf_op jit(solution)/shard_map/reduce_scatter | solution.py:54
  290.7 13.6 collective-permute-start.15
  322.1 85.7 %reduce-scatter.31.cloned.1.call-start = ((), (), s32[]{:S(2)}) async-start(), calls=%async_computation.25 | async-start | bytes 1310720 | tf_op jit(solution)/shard_map/reduce_scatter | solution.py:54
  350.3 13.6 collective-permute-start.18
  382.4 100.3 %reduce-scatter.33.cloned.1.call-start = ((), (), s32[]{:S(2)}) async-start(), calls=%async_computation.26 | async-start | bytes 1310720 | tf_op jit(solution)/shard_map/reduce_scatter | solution.py:54
  425.0 13.5 collective-permute-start.22
  456.3 99.8 %reduce-scatter.35.cloned.1.call-start = ((), (), s32[]{:S(2)}) async-start(), calls=%async_computation.27 | async-start | bytes 1310720 | tf_op jit(solution)/shard_map/reduce_scatter | solution.py:54
  484.6 13.6 collective-permute-start.25
  516.6 108.5 %reduce-scatter.37.cloned.1.call-start = ((), (), s32[]{:S(2)}) async-start(), calls=%async_computation.28 | async-start | bytes 1310720 | tf_op jit(solution)/shard_map/reduce_scatter | solution.py:54
  519.0 16.9 collective-permute-start.34
  519.0 24.8 %collective-permute-start.35 = (bf16[64,1,2048]{2,0,1:T(8,128)(2,1)}, bf16[64,1,2048]{2,0,1:T(8,128)(2,1)}, u32[]{:S(2)}, u32[]{:S(2)}) collective-permute-start(bf16[64,1,2048]{2,0,1:T(8,128)(2,1)} %get-tuple-element.203), channel_id=1, source_target_pairs={{0,12},{4,0},{8,4},{12,8},{1,13},{5,1},{9,5},{13,9},{2,14},{6,2},{... | collective-permute-start | bytes 786440 | tf_op jit(solution)/shard_map/ppermute | solution.py:21
  535.9 25.7 %collective-permute-start.36 = (bf16[64,1,2048]{2,0,1:T(8,128)(2,1)}, bf16[64,1,2048]{2,0,1:T(8,128)(2,1)}, u32[]{:S(2)}, u32[]{:S(2)}) collective-permute-start(bf16[64,1,2048]{2,0,1:T(8,128)(2,1)} %collective-permute-done.34), channel_id=1, source_target_pairs={{0,4},{4,8},{8,12},{12,0},{1,5},{5,9},{9,13},{13,1},{2,6},{6,10},{... | collective-permute-start | bytes 786440 | tf_op jit(solution)/shard_map/ppermute | solution.py:18
  570.3 13.4 collective-permute-start.29
  598.7 101.9 %reduce-scatter.41.cloned.1.call-start = ((), (), s32[]{:S(2)}) async-start(), calls=%async_computation.30 | async-start | bytes 1310720 | tf_op jit(solution)/shard_map/reduce_scatter | solution.py:54
  630.4 14.5 collective-permute-start.32
  675.2 100.7 %all-reduce.11.cloned.1.call-start = ((), (), s32[]{:S(2)}) async-start(), calls=%async_computation.32 | async-start | bytes 262144 | tf_op jit(solution)/shard_map/psum | solution.py:259
  711.0 13.8 collective-permute-start.38
  743.1 62.4 %reduce-scatter.43.cloned.1.call-start = ((), (), s32[]{:S(2)}) async-start(), calls=%async_computation.31 | async-start | bytes 1310720 | tf_op jit(solution)/shard_map/reduce_scatter | solution.py:54
  746.6 135.5 %reduce-scatter.45.cloned.1.call-start = ((), (), s32[]{:S(2)}) async-start(), calls=%async_computation.33 | async-start | bytes 1310720 | tf_op jit(solution)/shard_map/reduce_scatter | solution.py:54
  821.1 13.1 collective-permute-start.42
  857.5 100.8 %all-reduce.13.cloned.1.call-start = ((), (), s32[]{:S(2)}) async-start(), calls=%async_computation.35 | async-start | bytes 262144 | tf_op jit(solution)/shard_map/psum | solution.py:259
  892.3 13.8 collective-permute-start.45
  925.5 62.4 %reduce-scatter.47.cloned.1.call-start = ((), (), s32[]{:S(2)}) async-start(), calls=%async_computation.34 | async-start | bytes 1310720 | tf_op jit(solution)/shard_map/reduce_scatter | solution.py:54
  929.0 135.5 %reduce-scatter.49.cloned.1.call-start = ((), (), s32[]{:S(2)}) async-start(), calls=%async_computation.36 | async-start | bytes 1310720 | tf_op jit(solution)/shard_map/reduce_scatter | solution.py:54
  1003.6 13.1 collective-permute-start.49
  1040.0 100.8 %all-reduce.15.cloned.1.call-start = ((), (), s32[]{:S(2)}) async-start(), calls=%async_computation.38 | async-start | bytes 262144 | tf_op jit(solution)/shard_map/psum | solution.py:259
  1074.7 13.8 collective-permute-start.52
  1108.0 62.4 %reduce-scatter.51.cloned.1.call-start = ((), (), s32[]{:S(2)}) async-start(), calls=%async_computation.37 | async-start | bytes 1310720 | tf_op jit(solution)/shard_map/reduce_scatter | solution.py:54
  1111.5 129.8 %reduce-scatter.53.cloned.1.call-start = ((), (), s32[]{:S(2)}) async-start(), calls=%async_computation.39 | async-start | bytes 1310720 | tf_op jit(solution)/shard_map/reduce_scatter | solution.py:54
  1189.7 12.5 collective-permute-start.56
  1216.5 100.9 %all-reduce.17.cloned.1.call-start = ((), (), s32[]{:S(2)}) async-start(), calls=%async_computation.41 | async-start | bytes 262144 | tf_op jit(solution)/shard_map/psum | solution.py:259
  1251.5 13.8 collective-permute-start.59
  1284.7 62.5 %reduce-scatter.55.cloned.1.call-start = ((), (), s32[]{:S(2)}) async-start(), calls=%async_computation.40 | async-start | bytes 1310720 | tf_op jit(solution)/shard_map/reduce_scatter | solution.py:54
  1288.2 132.3 %reduce-scatter.57.cloned.1.call-start = ((), (), s32[]{:S(2)}) async-start(), calls=%async_computation.42 | async-start | bytes 1310720 | tf_op jit(solution)/shard_map/reduce_scatter | solution.py:54
  1364.0 14.1 collective-permute-start.63
  1396.0 244.9 %all-reduce.19.cloned.1.call-start = ((), (), s32[]{:S(2)}) async-start(), calls=%async_computation.44 | async-start | bytes 262144 | tf_op jit(solution)/shard_map/psum | solution.py:259
  1428.6 14.1 collective-permute-start.66
  1460.1 187.6 %reduce-scatter.39.cloned.1.call-start = ((), (), s32[]{:S(2)}) async-start(), calls=%async_computation.29 | async-start | bytes 1310720 | tf_op jit(solution)/shard_map/reduce_scatter | solution.py:54
  1469.9 202.6 %reduce-scatter.59.cloned.1.call-start = ((), (), s32[]{:S(2)}) async-start(), calls=%async_computation.43 | async-start | bytes 1310720 | tf_op jit(solution)/shard_map/reduce_scatter | solution.py:54
  1599.9 420.5 %all-reduce.21.cloned.1.call-start = ((), (), s32[]{:S(2)}) async-start(), calls=%async_computation.45 | async-start | bytes 44040192 | tf_op jit(solution)/shard_map/psum | solution.py:300
  (295 other events, 4096.7 us)
Sparse Core Ops, SparseCore 0:
  47.2 26.4 reduce-scatter.20
  114.9 25.2 reduce-scatter.22
  188.1 26.2 reduce-scatter.24
  248.4 25.3 reduce-scatter.26
  322.2 26.2 reduce-scatter.28
  382.5 25.2 reduce-scatter.30
  456.5 26.1 reduce-scatter.32
  516.7 39.3 reduce-scatter.34
  598.8 26.2 reduce-scatter.36
  675.3 25.2 reduce-scatter.40
  743.2 32.6 all-reduce.10
  778.7 26.7 reduce-scatter.42
  857.6 24.3 reduce-scatter.44
  925.6 32.6 all-reduce.12
  961.0 26.7 reduce-scatter.46
  1040.1 24.3 reduce-scatter.48
  1108.1 32.6 all-reduce.14
  1143.6 26.7 reduce-scatter.50
  1216.6 24.5 reduce-scatter.52
  1284.8 32.6 all-reduce.16
  1320.3 26.8 reduce-scatter.54
  1396.1 24.3 reduce-scatter.56
  1460.3 32.5 all-reduce.18
  1495.1 26.7 reduce-scatter.38
  1600.1 25.2 reduce-scatter.58
  1646.0 374.4 all-reduce.20
